TPU v7x, 32 devices: a whole 2x2x4 slice. The times are simulated.
32 devices in a mesh: parts: 2 (over y), gx: 4 (over z), gy: 4 (over x, core).
Axes of the slice: x: 2, y: 2, z: 4, core: 2. Of those that a mesh axis runs over, the one named last changes fastest.
Arguments:
- base_cond: float32 [3, 4, 32, 512], P(None, None, 'gx', 'gy'), may hold values from 0.5 to 2
- base_mass: float32 [4, 32, 512], P(None, 'gx', 'gy'), may hold values from 0.05 to 0.5
- fine_residual: float32 [8, 32, 512], P('parts', 'gx', 'gy'), parts along dimension 0, may hold values from -6 to 6
- point_index: int32 [2], P('parts'), parts along dimension 0, may hold values from 0 to 1048575
- gen_vector: int32 [32], replicated, may hold values from 1 to 1048575
- z_offset: int32 [1], replicated, may hold values from 0 to 508
Outputs:
- coarse_stencil: float32 [27, 4, 16, 256], P(None, 'parts', 'gx', 'gy'), parts along dimension 1
- coarse_solution: float32 [4, 16, 256], P('parts', 'gx', 'gy'), parts along dimension 0
There are 2 independent parts, one for each index of `parts`. A program takes and returns all parts, laid end to end along the dimension named above; an argument that names none is the same for every part. Nothing has to cross between parts.
All inputs are finite; a program needn't handle non-finite values.
Results may differ from a plain program's by a relative error of at most 0.0003.
Values sent between devices are 32-bit elements; how exact they have to be, the bound alone decides.
No kernel may reach another device: no remote copies, remote signals or barrier semaphores. Data moves between devices by JAX's collectives and lax.ppermute only.
A program may use at most 128 MiB of HBM per device.

v0:
```python
import math

import jax
import jax.numpy as jnp
from jax import lax
from jax.sharding import PartitionSpec as P

NZG = 512
QMCN = 1048576
SWEEPS = 4


omega_value = 0.6


def from_behind(value, axis, steps):
    count = lax.axis_size(axis)
    leading, last = (max(0, -steps), min(count, count - steps))
    return lax.ppermute(value, axis, [(source, source + steps) for source in range(leading, last)])


def extended(block, sides, width):
    for axis, dim in sides:
        count = lax.axis_size(axis)
        forward = [(i, i + 1) for i in range(count - 1)]
        backward = [(target, source) for source, target in forward]
        low = lax.ppermute(
            lax.slice_in_dim(block, block.shape[dim] - width, None, axis=dim), axis, forward
        )
        high = lax.ppermute(lax.slice_in_dim(block, 0, width, axis=dim), axis, backward)
        block = jnp.concatenate([low, block, high], axis=dim)
    return block


def lattice_shift(point_index, gen_vector):
    product = point_index[0] * gen_vector
    return jnp.remainder(product, QMCN).astype(jnp.float32) / QMCN - 0.5


def field_log(qmc_shift, x_glob, y_glob, z_glob, nx_total, ny_total):
    x_angle = (x_glob.astype(jnp.float32) + 0.5) * (math.pi / nx_total)
    y_angle = (y_glob.astype(jnp.float32) + 0.5) * (math.pi / ny_total)
    z_angle = (z_glob.astype(jnp.float32) + 0.5) * (math.pi / NZG)
    summed = jnp.zeros((z_glob.shape[0], x_glob.shape[0], y_glob.shape[0]), jnp.float32)
    for mode_index in range(qmc_shift.shape[0]):
        amplitude = 1.2 / (1.0 + 0.5 * mode_index)
        angle_sum = (z_angle * (mode_index % 5))[:, None, None] + (x_angle * (1 + mode_index % 4))[
            None, :, None
        ]
        angle_sum = (
            angle_sum + (y_angle * (1 + mode_index // 4 % 4))[None, None, :] + 0.7 * mode_index
        )
        summed = summed + qmc_shift[mode_index] * amplitude * jnp.cos(angle_sum)
    return summed


def effective(base_cond, base_mass, qmc_shift, x_glob, y_glob, z_local, z_base, nx_total, ny_total):
    z_glob = z_local + z_base
    log_here = field_log(qmc_shift, x_glob, y_glob, z_glob, nx_total, ny_total)
    log_east = field_log(qmc_shift, x_glob + 1, y_glob, z_glob, nx_total, ny_total)
    log_north = field_log(qmc_shift, x_glob, y_glob + 1, z_glob, nx_total, ny_total)
    log_upper = field_log(qmc_shift, x_glob, y_glob, z_glob + 1, nx_total, ny_total)
    open_x = (x_glob + 1 < nx_total)[None, :, None]
    open_y = (y_glob + 1 < ny_total)[None, None, :]
    open_z = (z_local + 1 < z_local.shape[0])[:, None, None]
    cond_x = jnp.where(open_x, base_cond[0] * jnp.exp(0.5 * (log_here + log_east)), 0.0)
    cond_y = jnp.where(open_y, base_cond[1] * jnp.exp(0.5 * (log_here + log_north)), 0.0)
    cond_z = jnp.where(open_z, base_cond[2] * jnp.exp(0.5 * (log_here + log_upper)), 0.0)
    mass_term = base_mass * jnp.exp(log_here)
    return jnp.stack([cond_x, cond_y, cond_z, mass_term])


def assemble(values, lower_x, lower_y):
    lead = [(0, 0)] * (values.ndim - 2)
    column = jnp.concatenate([lower_x, values], values.ndim - 2)
    side = jnp.pad(lower_y, lead + [(1, 0), (0, 0)])
    joined = jnp.concatenate([side, column], values.ndim - 1)
    return jnp.pad(joined, lead + [(0, 1), (0, 1)])


def couple(padded, cond_wide):
    cond_east = cond_wide[0, :, 1:-1, 1:-1]
    cond_west = cond_wide[0, :, :-2, 1:-1]
    cond_north = cond_wide[1, :, 1:-1, 1:-1]
    cond_south = cond_wide[1, :, 1:-1, :-2]
    cond_upper = cond_wide[2, :, 1:-1, 1:-1]
    cond_lower = jnp.pad(cond_upper, ((1, 0), (0, 0), (0, 0)))[:-1]
    middle = padded[..., 1:-1, 1:-1]
    lead = [(0, 0)] * (middle.ndim - 3)
    below = jnp.pad(middle, lead + [(1, 0), (0, 0), (0, 0)])[..., :-1, :, :]
    above = jnp.pad(middle, lead + [(0, 1), (0, 0), (0, 0)])[..., 1:, :, :]
    summed = cond_west * padded[..., :-2, 1:-1] + cond_east * padded[..., 2:, 1:-1]
    summed = summed + cond_south * padded[..., 1:-1, :-2] + cond_north * padded[..., 1:-1, 2:]
    return summed + cond_lower * below + cond_upper * above


def weights(cond_wide, x_glob, y_glob, z_local, nx_total, ny_total):
    cond_east = cond_wide[0, :, 1:-1, 1:-1]
    cond_west = cond_wide[0, :, :-2, 1:-1]
    cond_north = cond_wide[1, :, 1:-1, 1:-1]
    cond_south = cond_wide[1, :, 1:-1, :-2]
    cond_upper = cond_wide[2, :, 1:-1, 1:-1]
    cond_lower = jnp.pad(cond_upper, ((1, 0), (0, 0), (0, 0)))[:-1]
    mass_term = cond_wide[3, :, 1:-1, 1:-1]
    odd_x = (x_glob % 2 == 1)[None, :, None]
    odd_y = (y_glob % 2 == 1)[None, None, :]
    odd_z = (z_local % 2 == 1)[:, None, None]
    inside = ((x_glob >= 0) & (x_glob < nx_total))[None, :, None] & (
        (y_glob >= 0) & (y_glob < ny_total)
    )[None, None, :]
    pair_x = cond_east + cond_west
    pair_y = cond_north + cond_south
    pair_z = cond_upper + cond_lower
    denominator = (
        mass_term
        + jnp.where(odd_x, pair_x, 0.0)
        + jnp.where(odd_y, pair_y, 0.0)
        + jnp.where(odd_z, pair_z, 0.0)
    )
    reciprocal = jnp.where(inside, 1.0 / jnp.where(inside, denominator, 1.0), 0.0)
    odd_count = odd_x.astype(jnp.int32) + odd_y.astype(jnp.int32) + odd_z.astype(jnp.int32)
    weight_one = jnp.where(odd_count == 1, reciprocal, 0.0)
    weight_two = jnp.where(odd_count == 2, reciprocal, 0.0)
    weight_three = jnp.where(odd_count == 3, reciprocal, 0.0)
    diagonal = mass_term + pair_x + pair_y + pair_z
    return (weight_one, weight_two, weight_three, diagonal)


def prolong_apply(seed_wide, cond_wide, weight_one, weight_two, weight_three, diagonal, spread):
    level_zero = seed_wide[..., 1:-1, 1:-1]
    level_one = level_zero + weight_one * couple(seed_wide, cond_wide)
    level_two = level_one + weight_two * couple(spread(level_one), cond_wide)
    level_three = level_two + weight_three * couple(spread(level_two), cond_wide)
    return diagonal * level_three - couple(spread(level_three), cond_wide)


def restrict(applied, cond_wide, weight_one, weight_two, weight_three, spread):
    applied = applied + couple(spread(weight_three * applied), cond_wide)
    applied = applied + couple(spread(weight_two * applied), cond_wide)
    return applied + couple(spread(weight_one * applied), cond_wide)


def colour_table(coords, upper_limit):
    usable = (coords % 2 == 0) & (coords >= 0) & (coords < upper_limit)
    colour_of = coords // 2 % 3
    return jnp.stack(
        [jnp.where(usable & (colour_of == colour), 1.0, 0.0) for colour in range(3)]
    ).astype(jnp.float32)


def offset_table(coords):
    return jnp.stack(
        [
            jnp.stack(
                [jnp.where((coords + offset - 1) % 3 == colour, 1.0, 0.0) for colour in range(3)]
            )
            for offset in range(3)
        ]
    ).astype(jnp.float32)


def select_offsets(probes, q_z, q_x, q_y):
    table_z = offset_table(q_z)
    table_x = offset_table(q_x)
    table_y = offset_table(q_y)
    plane_count, size_x, size_y = probes.shape[1:]
    grouped = probes.reshape(3, 3, 3, plane_count, size_x, size_y)
    section_one = jnp.sum(table_z[:, :, None, None, :, None, None] * grouped[None], axis=1)
    section_two = jnp.sum(table_x[None, :, :, None, None, :, None] * section_one[:, None], axis=2)
    section_three = jnp.sum(
        table_y[None, None, :, :, None, None, :] * section_two[:, :, None], axis=3
    )
    return section_three.reshape(27, plane_count, size_x, size_y)


def apply_coarse(stencil, padded):
    plane_count, size_x, size_y = stencil.shape[1:]
    deep_pad = jnp.pad(padded, ((1, 1), (0, 0), (0, 0)))
    summed = jnp.zeros((plane_count, size_x, size_y), jnp.float32)
    for offset_z in range(3):
        for offset_x in range(3):
            for offset_y in range(3):
                summed = (
                    summed
                    + stencil[9 * offset_z + 3 * offset_x + offset_y]
                    * deep_pad[
                        offset_z : offset_z + plane_count,
                        offset_x : offset_x + size_x,
                        offset_y : offset_y + size_y,
                    ]
                )
    return summed


def jacobi(stencil, coarse_rhs, diag_safe, spread):
    solution = omega_value * coarse_rhs / diag_safe
    for sweep_index in range(SWEEPS - 1):
        solution = (
            solution
            + omega_value * (coarse_rhs - apply_coarse(stencil, spread(solution))) / diag_safe
        )
    return solution


def on_device(base_cond, base_mass, fine_residual, point_index, gen_vector, z_offset):
    plane_count, width_x, width_y = base_mass.shape
    nx_total = width_x * lax.axis_size("gx")
    ny_total = width_y * lax.axis_size("gy")
    x_first = lax.axis_index("gx") * width_x
    y_first = lax.axis_index("gy") * width_y
    z_local = jnp.arange(plane_count, dtype=jnp.int32)
    qmc_shift = lattice_shift(point_index, gen_vector)
    x_own = x_first + jnp.arange(width_x, dtype=jnp.int32)
    y_own = y_first + jnp.arange(width_y, dtype=jnp.int32)
    coeffs = effective(
        base_cond, base_mass, qmc_shift, x_own, y_own, z_local, z_offset[0], nx_total, ny_total
    )
    margin = 0
    lower_x = from_behind(coeffs[0:1, :, -1:, :], "gx", 1)
    lower_y = from_behind(coeffs[1:2, :, :, -1:], "gy", 1)
    lower_x = jnp.pad(lower_x, ((0, 3), (0, 0), (0, 0), (0, 0)))
    lower_y = jnp.pad(lower_y, ((1, 2), (0, 0), (0, 0), (0, 0)))
    cond_wide = assemble(coeffs, lower_x, lower_y)

    def spread_forward(values):
        return extended(values, (("gx", 2), ("gy", 3)), 1)

    def spread_backward(values):
        below_x = from_behind(values[..., -1:, :], "gx", 1)
        below_y = from_behind(values[..., :, -1:], "gy", 1)
        return assemble(values, below_x, below_y)

    weight_one, weight_two, weight_three, diagonal = weights(
        cond_wide, x_own, y_own, z_local, nx_total, ny_total
    )
    x_wide = x_own[0] - 1 + jnp.arange(x_own.shape[0] + 2, dtype=jnp.int32)
    y_wide = y_own[0] - 1 + jnp.arange(y_own.shape[0] + 2, dtype=jnp.int32)
    table_z = colour_table(z_local, plane_count)
    table_x = colour_table(x_wide, nx_total)
    table_y = colour_table(y_wide, ny_total)
    seed_wide = (
        table_z[:, None, None, :, None, None]
        * table_x[None, :, None, None, :, None]
        * table_y[None, None, :, None, None, :]
    ).reshape(27, plane_count, x_wide.shape[0], y_wide.shape[0])
    applied = prolong_apply(
        seed_wide, cond_wide, weight_one, weight_two, weight_three, diagonal, spread_forward
    )
    restricted = jnp.concatenate([applied, fine_residual[None]], 0)
    restricted = restrict(
        restricted, cond_wide, weight_one, weight_two, weight_three, spread_backward
    )
    coarse = restricted[:, ::2, margin : margin + width_x : 2, margin : margin + width_y : 2]
    coarse_rhs = coarse[27]
    half_x = width_x // 2
    half_y = width_y // 2
    q_x = lax.axis_index("gx") * half_x + jnp.arange(half_x, dtype=jnp.int32)
    q_y = lax.axis_index("gy") * half_y + jnp.arange(half_y, dtype=jnp.int32)
    q_z = jnp.arange(plane_count // 2, dtype=jnp.int32)
    stencil = select_offsets(coarse[:27], q_z, q_x, q_y)

    def spread_grid(values):
        return extended(values, (("gx", 1), ("gy", 2)), 1)

    solution = jacobi(stencil, coarse_rhs, stencil[13], spread_grid)
    return (stencil, solution)


def solution(mesh):
    return jax.shard_map(
        on_device,
        mesh=mesh,
        in_specs=(
            P(None, None, "gx", "gy"),
            P(None, "gx", "gy"),
            P("parts", "gx", "gy"),
            P("parts"),
            P(),
            P(),
        ),
        out_specs=(P(None, "parts", "gx", "gy"), P("parts", "gx", "gy")),
        check_vma=False,
    )
```

profile of v0, /device:TPU:1, one launch (start us, length us, event | category | flops | bytes accessed | tf_op | source)
XLA Modules:
  0.0 195.9 jit_solution(15490928142778224511)
XLA Ops:
  24.3 4.4 %multiply_select_fusion.2 = (f32[1,4,8,128]{3,2,1,0:T(8,128)S(1)}, f32[1,4,8,128]{3,2,1,0:T(8,128)S(1)}) fusion(f32[3,4,8,128]{3,2,1,0:T(8,128)} %param.6, f32[4,8]{1,0:T(4,128)S(1)} %get-tuple-element.103, f32[4,8]{1,0:T(4,128)S(1)} %get-tuple-element.94, f32[4,8]{1,0:T(4,128)S(1)} %get-tuple-element.80, f32[4,8]{1,0:T(4,128)S(1)} %get-tuple-element.89, ...), kind=kLoop, calls=%fused_computation.184 | loop fusion | flops 1048576 | bytes 56456 | tf_op jit(solution)/shard_map/jit(_where)/select_n | solution.py:66
  31.5 4.5 %collective-permute-start.1 = (f32[1,4,8,1]{3,2,1,0:T(8,128)S(1)}, f32[1,4,8,1]{3,2,1,0:T(8,128)S(1)}, u32[]{:S(2)}, u32[]{:S(2)}) collective-permute-start(f32[1,4,8,1]{3,2,1,0:T(8,128)S(1)} %slice.1199), channel_id=1, source_target_pairs={{0,1},{1,2},{2,3},{4,5},{5,6},{6,7},{8,9},{9,10},{10,11},{12,13},{... | collective-permute-start | bytes 392 | tf_op jit(solution)/shard_map/ppermute | solution.py:19
  36.0 3.4 %collective-permute-start = (f32[1,4,1,128]{3,2,1,0:T(1,128)S(1)}, f32[1,4,1,128]{3,2,1,0:T(1,128)S(1)}, u32[]{:S(2)}, u32[]{:S(2)}) collective-permute-start(f32[1,4,1,128]{3,2,1,0:T(1,128)S(1)} %slice.1198), channel_id=1, source_target_pairs={{0,4},{4,8},{8,12},{1,5},{5,9},{9,13},{2,6},{6,10},{10,14},{3,7},{... | collective-permute-start | bytes 6152 | tf_op jit(solution)/shard_map/ppermute | solution.py:19
  51.8 3.2 %collective-permute-start.2 = (f32[27,4,1,128]{3,1,2,0:T(4,128)S(1)}, f32[27,4,1,128]{3,1,2,0:T(4,128)S(1)}, u32[]{:S(2)}, u32[]{:S(2)}) collective-permute-start(f32[27,4,1,128]{3,1,2,0:T(4,128)S(1)} %get-tuple-element.25), channel_id=1, source_target_pairs={{0,4},{4,8},{8,12},{1,5},{5,9},{9,13},{2,6},{6,10},{10,14},{3,7},{... | collective-permute-start | bytes 165896 | tf_op jit(solution)/shard_map/ppermute | solution.py:27
  56.3 4.0 %collective-permute-done.3 = f32[27,4,1,128]{3,1,2,0:T(4,128)S(1)} collective-permute-done((f32[27,4,1,128]{3,1,2,0:T(4,128)S(1)}, f32[27,4,1,128]{3,1,2,0:T(4,128)S(1)}, u32[]{:S(2)}, u32[]{:S(2)}) %collective-permute-start.3) | collective-permute-done | bytes 55328 | tf_op jit(solution)/shard_map/ppermute | solution.py:30
  61.2 3.2 %collective-permute-start.4 = (f32[27,4,10,1]{0,1,3,2:T(4,128)S(1)}, f32[27,4,10,1]{0,1,3,2:T(4,128)S(1)}, u32[]{:S(2)}, u32[]{:S(2)}) collective-permute-start(f32[27,4,10,1]{0,1,3,2:T(4,128)S(1)} %copy.127), channel_id=1, source_target_pairs={{0,1},{1,2},{2,3},{4,5},{5,6},{6,7},{8,9},{9,10},{10,11},{12,13},{... | collective-permute-start | bytes 12968 | tf_op jit(solution)/shard_map/ppermute | solution.py:27
  71.2 3.2 %collective-permute-start.6 = (f32[27,4,1,128]{3,1,2,0:T(4,128)S(1)}, f32[27,4,1,128]{3,1,2,0:T(4,128)S(1)}, u32[]{:S(2)}, u32[]{:S(2)}) collective-permute-start(f32[27,4,1,128]{3,1,2,0:T(4,128)S(1)} %get-tuple-element.23), channel_id=1, source_target_pairs={{0,4},{4,8},{8,12},{1,5},{5,9},{9,13},{2,6},{6,10},{10,14},{3,7},{... | collective-permute-start | bytes 165896 | tf_op jit(solution)/shard_map/ppermute | solution.py:27
  75.8 3.6 %collective-permute-done.7 = f32[27,4,1,128]{3,1,2,0:T(4,128)S(1)} collective-permute-done((f32[27,4,1,128]{3,1,2,0:T(4,128)S(1)}, f32[27,4,1,128]{3,1,2,0:T(4,128)S(1)}, u32[]{:S(2)}, u32[]{:S(2)}) %collective-permute-start.7) | collective-permute-done | bytes 55328 | tf_op jit(solution)/shard_map/ppermute | solution.py:30
  80.2 3.4 %collective-permute-start.8 = (f32[27,4,10,1]{0,1,3,2:T(4,128)S(1)}, f32[27,4,10,1]{0,1,3,2:T(4,128)S(1)}, u32[]{:S(2)}, u32[]{:S(2)}) collective-permute-start(f32[27,4,10,1]{0,1,3,2:T(4,128)S(1)} %copy.129), channel_id=1, source_target_pairs={{0,1},{1,2},{2,3},{4,5},{5,6},{6,7},{8,9},{9,10},{10,11},{12,13},{... | collective-permute-start | bytes 12968 | tf_op jit(solution)/shard_map/ppermute | solution.py:27
  93.4 3.6 %collective-permute-done.11 = f32[27,4,1,128]{3,1,2,0:T(4,128)S(1)} collective-permute-done((f32[27,4,1,128]{3,1,2,0:T(4,128)S(1)}, f32[27,4,1,128]{3,1,2,0:T(4,128)S(1)}, u32[]{:S(2)}, u32[]{:S(2)}) %collective-permute-start.11) | collective-permute-done | bytes 55328 | tf_op jit(solution)/shard_map/ppermute | solution.py:30
  97.8 3.4 %collective-permute-start.12 = (f32[27,4,10,1]{0,1,3,2:T(4,128)S(1)}, f32[27,4,10,1]{0,1,3,2:T(4,128)S(1)}, u32[]{:S(2)}, u32[]{:S(2)}) collective-permute-start(f32[27,4,10,1]{0,1,3,2:T(4,128)S(1)} %copy.131), channel_id=1, source_target_pairs={{0,1},{1,2},{2,3},{4,5},{5,6},{6,7},{8,9},{9,10},{10,11},{12,13},{... | collective-permute-start | bytes 12968 | tf_op jit(solution)/shard_map/ppermute | solution.py:27
  112.1 3.7 %collective-permute-done.15 = f32[28,4,8,1]{3,2,1,0:T(8,128)S(1)} collective-permute-done((f32[28,4,8,1]{3,2,1,0:T(8,128)S(1)}, f32[28,4,8,1]{3,2,1,0:T(8,128)S(1)}, u32[]{:S(2)}, u32[]{:S(2)}) %collective-permute-start.15) | collective-permute-done | bytes 3616 | tf_op jit(solution)/shard_map/ppermute | solution.py:19
  117.3 4.4 %collective-permute-start.17 = (f32[28,4,8,1]{3,2,1,0:T(8,128)S(1)}, f32[28,4,8,1]{3,2,1,0:T(8,128)S(1)}, u32[]{:S(2)}, u32[]{:S(2)}) collective-permute-start(f32[28,4,8,1]{3,2,1,0:T(8,128)S(1)} %slice.1221), channel_id=1, source_target_pairs={{0,1},{1,2},{2,3},{4,5},{5,6},{6,7},{8,9},{9,10},{10,11},{12,13},{... | collective-permute-start | bytes 10760 | tf_op jit(solution)/shard_map/ppermute | solution.py:19
  123.5 3.7 %collective-permute-done.17 = f32[28,4,8,1]{3,2,1,0:T(8,128)S(1)} collective-permute-done((f32[28,4,8,1]{3,2,1,0:T(8,128)S(1)}, f32[28,4,8,1]{3,2,1,0:T(8,128)S(1)}, u32[]{:S(2)}, u32[]{:S(2)}) %collective-permute-start.17) | collective-permute-done | bytes 3616 | tf_op jit(solution)/shard_map/ppermute | solution.py:19
  128.7 4.4 %collective-permute-start.19 = (f32[28,4,8,1]{3,2,1,0:T(8,128)S(1)}, f32[28,4,8,1]{3,2,1,0:T(8,128)S(1)}, u32[]{:S(2)}, u32[]{:S(2)}) collective-permute-start(f32[28,4,8,1]{3,2,1,0:T(8,128)S(1)} %slice.1224), channel_id=1, source_target_pairs={{0,1},{1,2},{2,3},{4,5},{5,6},{6,7},{8,9},{9,10},{10,11},{12,13},{... | collective-permute-start | bytes 10760 | tf_op jit(solution)/shard_map/ppermute | solution.py:19
  135.1 3.4 %collective-permute-done.19 = f32[28,4,8,1]{3,2,1,0:T(8,128)S(1)} collective-permute-done((f32[28,4,8,1]{3,2,1,0:T(8,128)S(1)}, f32[28,4,8,1]{3,2,1,0:T(8,128)S(1)}, u32[]{:S(2)}, u32[]{:S(2)}) %collective-permute-start.19) | collective-permute-done | bytes 3616 | tf_op jit(solution)/shard_map/ppermute | solution.py:19
  139.8 8.5 %slice.1078 = f32[28,2,4,64]{3,2,1,0:T(4,128)S(1)} slice(f32[28,4,8,128]{3,2,1,0:T(8,128)S(1)} %fusion.13), slice={[0:28:1], [0:4:2], [0:8:2], [0:128:2]} | slice | bytes 114688 | tf_op jit(solution)/shard_map/slice | solution.py:253
  154.9 5.8 %collective-permute-start.22 = (f32[2,6,1]{2,1,0:T(8,128)S(1)}, f32[2,6,1]{2,1,0:T(8,128)S(1)}, u32[]{:S(2)}, u32[]{:S(2)}) collective-permute-start(f32[2,6,1]{2,1,0:T(8,128)S(1)} %get-tuple-element.34), channel_id=1, source_target_pairs={{0,1},{1,2},{2,3},{4,5},{5,6},{6,7},{8,9},{9,10},{10,11},{12,13},{... | collective-permute-start | bytes 152 | tf_op jit(solution)/shard_map/ppermute | solution.py:27
  162.6 3.0 %collective-permute-done.23 = f32[2,6,1]{2,1,0:T(8,128)S(1)} collective-permute-done((f32[2,6,1]{2,1,0:T(8,128)S(1)}, f32[2,6,1]{2,1,0:T(8,128)S(1)}, u32[]{:S(2)}, u32[]{:S(2)}) %collective-permute-start.23) | collective-permute-done | bytes 80 | tf_op jit(solution)/shard_map/ppermute | solution.py:30
  168.9 3.0 %collective-permute-done.25 = f32[2,1,64]{2,1,0:T(1,128)S(1)} collective-permute-done((f32[2,1,64]{2,1,0:T(1,128)S(1)}, f32[2,1,64]{2,1,0:T(1,128)S(1)}, u32[]{:S(2)}, u32[]{:S(2)}) %collective-permute-start.25) | collective-permute-done | bytes 544 | tf_op jit(solution)/shard_map/ppermute | solution.py:30
  172.0 3.4 %collective-permute-start.26 = (f32[2,6,1]{2,1,0:T(8,128)S(1)}, f32[2,6,1]{2,1,0:T(8,128)S(1)}, u32[]{:S(2)}, u32[]{:S(2)}) collective-permute-start(f32[2,6,1]{2,1,0:T(8,128)S(1)} %get-tuple-element.32), channel_id=1, source_target_pairs={{0,1},{1,2},{2,3},{4,5},{5,6},{6,7},{8,9},{9,10},{10,11},{12,13},{... | collective-permute-start | bytes 152 | tf_op jit(solution)/shard_map/ppermute | solution.py:27
  177.3 3.0 %collective-permute-done.27 = f32[2,6,1]{2,1,0:T(8,128)S(1)} collective-permute-done((f32[2,6,1]{2,1,0:T(8,128)S(1)}, f32[2,6,1]{2,1,0:T(8,128)S(1)}, u32[]{:S(2)}, u32[]{:S(2)}) %collective-permute-start.27) | collective-permute-done | bytes 80 | tf_op jit(solution)/shard_map/ppermute | solution.py:30
  186.7 3.4 %collective-permute-start.30 = (f32[2,6,1]{2,1,0:T(8,128)S(1)}, f32[2,6,1]{2,1,0:T(8,128)S(1)}, u32[]{:S(2)}, u32[]{:S(2)}) collective-permute-start(f32[2,6,1]{2,1,0:T(8,128)S(1)} %get-tuple-element.30), channel_id=1, source_target_pairs={{0,1},{1,2},{2,3},{4,5},{5,6},{6,7},{8,9},{9,10},{10,11},{12,13},{... | collective-permute-start | bytes 152 | tf_op jit(solution)/shard_map/ppermute | solution.py:27
  192.0 3.0 %collective-permute-done.31 = f32[2,6,1]{2,1,0:T(8,128)S(1)} collective-permute-done((f32[2,6,1]{2,1,0:T(8,128)S(1)}, f32[2,6,1]{2,1,0:T(8,128)S(1)}, u32[]{:S(2)}, u32[]{:S(2)}) %collective-permute-start.31) | collective-permute-done | bytes 80 | tf_op jit(solution)/shard_map/ppermute | solution.py:30
  (203 shorter events, 80.5 us)
Async XLA Ops:
  31.5 15.3 %collective-permute-start.1 = (f32[1,4,8,1]{3,2,1,0:T(8,128)S(1)}, f32[1,4,8,1]{3,2,1,0:T(8,128)S(1)}, u32[]{:S(2)}, u32[]{:S(2)}) collective-permute-start(f32[1,4,8,1]{3,2,1,0:T(8,128)S(1)} %slice.1199), channel_id=1, source_target_pairs={{0,1},{1,2},{2,3},{4,5},{5,6},{6,7},{8,9},{9,10},{10,11},{12,13},{... | collective-permute-start | bytes 392 | tf_op jit(solution)/shard_map/ppermute | solution.py:19
  36.0 10.7 %collective-permute-start = (f32[1,4,1,128]{3,2,1,0:T(1,128)S(1)}, f32[1,4,1,128]{3,2,1,0:T(1,128)S(1)}, u32[]{:S(2)}, u32[]{:S(2)}) collective-permute-start(f32[1,4,1,128]{3,2,1,0:T(1,128)S(1)} %slice.1198), channel_id=1, source_target_pairs={{0,4},{4,8},{8,12},{1,5},{5,9},{9,13},{2,6},{6,10},{10,14},{3,7},{... | collective-permute-start | bytes 6152 | tf_op jit(solution)/shard_map/ppermute | solution.py:19
  55.0 5.3 %collective-permute-start.3 = (f32[27,4,1,128]{3,1,2,0:T(4,128)S(1)}, f32[27,4,1,128]{3,1,2,0:T(4,128)S(1)}, u32[]{:S(2)}, u32[]{:S(2)}) collective-permute-start(f32[27,4,1,128]{3,1,2,0:T(4,128)S(1)} %get-tuple-element.26), channel_id=1, source_target_pairs={{4,0},{8,4},{12,8},{5,1},{9,5},{13,9},{6,2},{10,6},{14,10},{7,3},{... | collective-permute-start | bytes 165896 | tf_op jit(solution)/shard_map/ppermute | solution.py:30
  61.2 5.8 %collective-permute-start.4 = (f32[27,4,10,1]{0,1,3,2:T(4,128)S(1)}, f32[27,4,10,1]{0,1,3,2:T(4,128)S(1)}, u32[]{:S(2)}, u32[]{:S(2)}) collective-permute-start(f32[27,4,10,1]{0,1,3,2:T(4,128)S(1)} %copy.127), channel_id=1, source_target_pairs={{0,1},{1,2},{2,3},{4,5},{5,6},{6,7},{8,9},{9,10},{10,11},{12,13},{... | collective-permute-start | bytes 12968 | tf_op jit(solution)/shard_map/ppermute | solution.py:27
  64.7 5.1 %collective-permute-start.5 = (f32[27,4,10,1]{0,1,3,2:T(4,128)S(1)}, f32[27,4,10,1]{0,1,3,2:T(4,128)S(1)}, u32[]{:S(2)}, u32[]{:S(2)}) collective-permute-start(f32[27,4,10,1]{0,1,3,2:T(4,128)S(1)} %copy.128), channel_id=1, source_target_pairs={{1,0},{2,1},{3,2},{5,4},{6,5},{7,6},{9,8},{10,9},{11,10},{13,12},{... | collective-permute-start | bytes 12968 | tf_op jit(solution)/shard_map/ppermute | solution.py:30
  71.2 4.5 %collective-permute-start.6 = (f32[27,4,1,128]{3,1,2,0:T(4,128)S(1)}, f32[27,4,1,128]{3,1,2,0:T(4,128)S(1)}, u32[]{:S(2)}, u32[]{:S(2)}) collective-permute-start(f32[27,4,1,128]{3,1,2,0:T(4,128)S(1)} %get-tuple-element.23), channel_id=1, source_target_pairs={{0,4},{4,8},{8,12},{1,5},{5,9},{9,13},{2,6},{6,10},{10,14},{3,7},{... | collective-permute-start | bytes 165896 | tf_op jit(solution)/shard_map/ppermute | solution.py:27
  74.5 4.9 %collective-permute-start.7 = (f32[27,4,1,128]{3,1,2,0:T(4,128)S(1)}, f32[27,4,1,128]{3,1,2,0:T(4,128)S(1)}, u32[]{:S(2)}, u32[]{:S(2)}) collective-permute-start(f32[27,4,1,128]{3,1,2,0:T(4,128)S(1)} %get-tuple-element.24), channel_id=1, source_target_pairs={{4,0},{8,4},{12,8},{5,1},{9,5},{13,9},{6,2},{10,6},{14,10},{7,3},{... | collective-permute-start | bytes 165896 | tf_op jit(solution)/shard_map/ppermute | solution.py:30
  80.2 5.7 %collective-permute-start.8 = (f32[27,4,10,1]{0,1,3,2:T(4,128)S(1)}, f32[27,4,10,1]{0,1,3,2:T(4,128)S(1)}, u32[]{:S(2)}, u32[]{:S(2)}) collective-permute-start(f32[27,4,10,1]{0,1,3,2:T(4,128)S(1)} %copy.129), channel_id=1, source_target_pairs={{0,1},{1,2},{2,3},{4,5},{5,6},{6,7},{8,9},{9,10},{10,11},{12,13},{... | collective-permute-start | bytes 12968 | tf_op jit(solution)/shard_map/ppermute | solution.py:27
  83.9 5.1 %collective-permute-start.9 = (f32[27,4,10,1]{0,1,3,2:T(4,128)S(1)}, f32[27,4,10,1]{0,1,3,2:T(4,128)S(1)}, u32[]{:S(2)}, u32[]{:S(2)}) collective-permute-start(f32[27,4,10,1]{0,1,3,2:T(4,128)S(1)} %copy.130), channel_id=1, source_target_pairs={{1,0},{2,1},{3,2},{5,4},{6,5},{7,6},{9,8},{10,9},{11,10},{13,12},{... | collective-permute-start | bytes 12968 | tf_op jit(solution)/shard_map/ppermute | solution.py:30
  92.1 4.9 %collective-permute-start.11 = (f32[27,4,1,128]{3,1,2,0:T(4,128)S(1)}, f32[27,4,1,128]{3,1,2,0:T(4,128)S(1)}, u32[]{:S(2)}, u32[]{:S(2)}) collective-permute-start(f32[27,4,1,128]{3,1,2,0:T(4,128)S(1)} %get-tuple-element.22), channel_id=1, source_target_pairs={{4,0},{8,4},{12,8},{5,1},{9,5},{13,9},{6,2},{10,6},{14,10},{7,3},{... | collective-permute-start | bytes 165896 | tf_op jit(solution)/shard_map/ppermute | solution.py:30
  97.8 5.7 %collective-permute-start.12 = (f32[27,4,10,1]{0,1,3,2:T(4,128)S(1)}, f32[27,4,10,1]{0,1,3,2:T(4,128)S(1)}, u32[]{:S(2)}, u32[]{:S(2)}) collective-permute-start(f32[27,4,10,1]{0,1,3,2:T(4,128)S(1)} %copy.131), channel_id=1, source_target_pairs={{0,1},{1,2},{2,3},{4,5},{5,6},{6,7},{8,9},{9,10},{10,11},{12,13},{... | collective-permute-start | bytes 12968 | tf_op jit(solution)/shard_map/ppermute | solution.py:27
  101.5 5.1 %collective-permute-start.13 = (f32[27,4,10,1]{0,1,3,2:T(4,128)S(1)}, f32[27,4,10,1]{0,1,3,2:T(4,128)S(1)}, u32[]{:S(2)}, u32[]{:S(2)}) collective-permute-start(f32[27,4,10,1]{0,1,3,2:T(4,128)S(1)} %copy.132), channel_id=1, source_target_pairs={{1,0},{2,1},{3,2},{5,4},{6,5},{7,6},{9,8},{10,9},{11,10},{13,12},{... | collective-permute-start | bytes 12968 | tf_op jit(solution)/shard_map/ppermute | solution.py:30
  108.4 7.3 %collective-permute-start.15 = (f32[28,4,8,1]{3,2,1,0:T(8,128)S(1)}, f32[28,4,8,1]{3,2,1,0:T(8,128)S(1)}, u32[]{:S(2)}, u32[]{:S(2)}) collective-permute-start(f32[28,4,8,1]{3,2,1,0:T(8,128)S(1)} %slice.1218), channel_id=1, source_target_pairs={{0,1},{1,2},{2,3},{4,5},{5,6},{6,7},{8,9},{9,10},{10,11},{12,13},{... | collective-permute-start | bytes 10760 | tf_op jit(solution)/shard_map/ppermute | solution.py:19
  110.4 5.4 %collective-permute-start.14 = (f32[28,4,1,128]{3,2,1,0:T(1,128)S(1)}, f32[28,4,1,128]{3,2,1,0:T(1,128)S(1)}, u32[]{:S(2)}, u32[]{:S(2)}) collective-permute-start(f32[28,4,1,128]{3,2,1,0:T(1,128)S(1)} %slice.1217), channel_id=1, source_target_pairs={{0,4},{4,8},{8,12},{1,5},{5,9},{9,13},{2,6},{6,10},{10,14},{3,7},{... | collective-permute-start | bytes 172040 | tf_op jit(solution)/shard_map/ppermute | solution.py:19
  117.3 9.8 %collective-permute-start.17 = (f32[28,4,8,1]{3,2,1,0:T(8,128)S(1)}, f32[28,4,8,1]{3,2,1,0:T(8,128)S(1)}, u32[]{:S(2)}, u32[]{:S(2)}) collective-permute-start(f32[28,4,8,1]{3,2,1,0:T(8,128)S(1)} %slice.1221), channel_id=1, source_target_pairs={{0,1},{1,2},{2,3},{4,5},{5,6},{6,7},{8,9},{9,10},{10,11},{12,13},{... | collective-permute-start | bytes 10760 | tf_op jit(solution)/shard_map/ppermute | solution.py:19
  121.7 5.4 %collective-permute-start.16 = (f32[28,4,1,128]{3,2,1,0:T(1,128)S(1)}, f32[28,4,1,128]{3,2,1,0:T(1,128)S(1)}, u32[]{:S(2)}, u32[]{:S(2)}) collective-permute-start(f32[28,4,1,128]{3,2,1,0:T(1,128)S(1)} %slice.1220), channel_id=1, source_target_pairs={{0,4},{4,8},{8,12},{1,5},{5,9},{9,13},{2,6},{6,10},{10,14},{3,7},{... | collective-permute-start | bytes 172040 | tf_op jit(solution)/shard_map/ppermute | solution.py:19
  128.7 9.8 %collective-permute-start.19 = (f32[28,4,8,1]{3,2,1,0:T(8,128)S(1)}, f32[28,4,8,1]{3,2,1,0:T(8,128)S(1)}, u32[]{:S(2)}, u32[]{:S(2)}) collective-permute-start(f32[28,4,8,1]{3,2,1,0:T(8,128)S(1)} %slice.1224), channel_id=1, source_target_pairs={{0,1},{1,2},{2,3},{4,5},{5,6},{6,7},{8,9},{9,10},{10,11},{12,13},{... | collective-permute-start | bytes 10760 | tf_op jit(solution)/shard_map/ppermute | solution.py:19
  133.1 5.4 %collective-permute-start.18 = (f32[28,4,1,128]{3,2,1,0:T(1,128)S(1)}, f32[28,4,1,128]{3,2,1,0:T(1,128)S(1)}, u32[]{:S(2)}, u32[]{:S(2)}) collective-permute-start(f32[28,4,1,128]{3,2,1,0:T(1,128)S(1)} %slice.1223), channel_id=1, source_target_pairs={{0,4},{4,8},{8,12},{1,5},{5,9},{9,13},{2,6},{6,10},{10,14},{3,7},{... | collective-permute-start | bytes 172040 | tf_op jit(solution)/shard_map/ppermute | solution.py:19
  154.9 7.7 %collective-permute-start.22 = (f32[2,6,1]{2,1,0:T(8,128)S(1)}, f32[2,6,1]{2,1,0:T(8,128)S(1)}, u32[]{:S(2)}, u32[]{:S(2)}) collective-permute-start(f32[2,6,1]{2,1,0:T(8,128)S(1)} %get-tuple-element.34), channel_id=1, source_target_pairs={{0,1},{1,2},{2,3},{4,5},{5,6},{6,7},{8,9},{9,10},{10,11},{12,13},{... | collective-permute-start | bytes 152 | tf_op jit(solution)/shard_map/ppermute | solution.py:27
  160.7 5.0 %collective-permute-start.23 = (f32[2,6,1]{2,1,0:T(8,128)S(1)}, f32[2,6,1]{2,1,0:T(8,128)S(1)}, u32[]{:S(2)}, u32[]{:S(2)}) collective-permute-start(f32[2,6,1]{2,1,0:T(8,128)S(1)} %get-tuple-element.35), channel_id=1, source_target_pairs={{1,0},{2,1},{3,2},{5,4},{6,5},{7,6},{9,8},{10,9},{11,10},{13,12},{... | collective-permute-start | bytes 152 | tf_op jit(solution)/shard_map/ppermute | solution.py:30
  172.0 5.3 %collective-permute-start.26 = (f32[2,6,1]{2,1,0:T(8,128)S(1)}, f32[2,6,1]{2,1,0:T(8,128)S(1)}, u32[]{:S(2)}, u32[]{:S(2)}) collective-permute-start(f32[2,6,1]{2,1,0:T(8,128)S(1)} %get-tuple-element.32), channel_id=1, source_target_pairs={{0,1},{1,2},{2,3},{4,5},{5,6},{6,7},{8,9},{9,10},{10,11},{12,13},{... | collective-permute-start | bytes 152 | tf_op jit(solution)/shard_map/ppermute | solution.py:27
  175.4 5.0 %collective-permute-start.27 = (f32[2,6,1]{2,1,0:T(8,128)S(1)}, f32[2,6,1]{2,1,0:T(8,128)S(1)}, u32[]{:S(2)}, u32[]{:S(2)}) collective-permute-start(f32[2,6,1]{2,1,0:T(8,128)S(1)} %get-tuple-element.33), channel_id=1, source_target_pairs={{1,0},{2,1},{3,2},{5,4},{6,5},{7,6},{9,8},{10,9},{11,10},{13,12},{... | collective-permute-start | bytes 152 | tf_op jit(solution)/shard_map/ppermute | solution.py:30
  186.7 5.3 %collective-permute-start.30 = (f32[2,6,1]{2,1,0:T(8,128)S(1)}, f32[2,6,1]{2,1,0:T(8,128)S(1)}, u32[]{:S(2)}, u32[]{:S(2)}) collective-permute-start(f32[2,6,1]{2,1,0:T(8,128)S(1)} %get-tuple-element.30), channel_id=1, source_target_pairs={{0,1},{1,2},{2,3},{4,5},{5,6},{6,7},{8,9},{9,10},{10,11},{12,13},{... | collective-permute-start | bytes 152 | tf_op jit(solution)/shard_map/ppermute | solution.py:27
  190.0 5.0 %collective-permute-start.31 = (f32[2,6,1]{2,1,0:T(8,128)S(1)}, f32[2,6,1]{2,1,0:T(8,128)S(1)}, u32[]{:S(2)}, u32[]{:S(2)}) collective-permute-start(f32[2,6,1]{2,1,0:T(8,128)S(1)} %get-tuple-element.31), channel_id=1, source_target_pairs={{1,0},{2,1},{3,2},{5,4},{6,5},{7,6},{9,8},{10,9},{11,10},{13,12},{... | collective-permute-start | bytes 152 | tf_op jit(solution)/shard_map/ppermute | solution.py:30
  (11 other events, 95.9 us)
where the time goes:
time: 197 us; the launch traced here: 196 us
  starting transfers between devices  78.7 us (40%)
  waiting for transfers between devices  47.9 us (24%)
  other arithmetic  29 us (15%)
  between operations  23 us (12%)
  local copies, waits for them, and re-layouts  17.3 us (9%)
    ppermute x12, waiting for transfers between devices, extended(): lax.ppermute(lax.slice_in_dim(block, 0, width, axis=dim), axis, backward)  37.2 us
    ppermute x12, starting transfers between devices, extended(): lax.ppermute(lax.slice_in_dim(block, block.shape[dim] - width, None, axis...  35.4 us
    ppermute x8, starting transfers between devices, from_behind(): lax.ppermute(value, axis, [(source, source + steps) for source in range(l...  23.8 us
    ppermute x12, starting transfers between devices, extended(): lax.ppermute(lax.slice_in_dim(block, 0, width, axis=dim), axis, backward)  19.5 us
    ppermute x8, waiting for transfers between devices, from_behind(): lax.ppermute(value, axis, [(source, source + steps) for source in range(l...  10.7 us
    slice x1, local copies, waits for them, and re-layouts, on_device(): restricted[:, ::2, margin:margin + width_x:2, margin:margin + width_y:2]  8.47 us
    select_n x1, other arithmetic, effective(): jnp.where(open_x, base_cond[0] * jnp.exp(0.5 * (log_here + log_east)), 0.0)  4.44 us
  transfers between devices with their start and end apart: 32, of which 15 were waited for; matrix products, arithmetic and copies ran while one was open for 5% of the time, Pallas kernels for 0%

commit v1 on v0

v1 whole, which is shorter than its diff:
```python
import math

import jax
import jax.numpy as jnp
from jax import lax
from jax.experimental import pallas as pl
from jax.experimental.pallas import tpu as pltpu
from jax.sharding import PartitionSpec as P

NZG = 512
QMCN = 1048576
SWEEPS = 4
OMEGA = 0.6
ROWS = 16
LANES = 128
HALO = 8
F32 = jnp.float32
BF16 = jnp.bfloat16


def iota(shape, dim):
    return lax.broadcasted_iota(jnp.int32, shape, dim)


def strips_body(cond_ref, mass_ref, resid_ref, low_ref, high_ref):
    width = cond_ref.shape[-1]
    row, lane = iota((HALO, width), 0), iota((HALO, width), 1)
    coeffs = jnp.concatenate([cond_ref[...].reshape(-1, width), mass_ref[...].reshape(-1, width)], 0)
    resid = resid_ref[...].reshape(-1, width)
    for out_ref, first in ((low_ref, 0), (high_ref, width - HALO)):
        pick = jnp.where(lane == row + first, 1.0, 0.0)
        for start, rows in ((0, coeffs), (HALO, resid)):
            taken = lax.dot_general(
                pick, rows, (((1,), (1,)), ((), ())), precision=lax.Precision.HIGHEST, preferred_element_type=F32
            )
            if rows.shape[0] < LANES:
                taken = jnp.concatenate([taken, jnp.zeros((HALO, LANES - rows.shape[0]), F32)], 1)
            out_ref[start : start + HALO, :] = taken


def field_body(nx_total, ny_total, width_x, width_y, point_ref, offset_ref, gen_ref, out_ref):
    modes = gen_ref.shape[1]
    x_first = lax.axis_index("gx") * width_x
    y_first = lax.axis_index("gy") * width_y
    half_x, half_y = width_x // 2, width_y // 2
    product = point_ref[0] * gen_ref[...]
    shift = (product & (QMCN - 1)).astype(F32) / QMCN - 0.5
    mode_row = iota((modes, modes), 0)
    mode_col = jnp.sum(jnp.where(mode_row == iota((modes, modes), 1), shift, 0.0), axis=1, keepdims=True)
    k = iota((modes, LANES), 0)
    lane = iota((modes, LANES), 1)
    k_f = k.astype(F32)
    amplitude = 1.2 / (1.0 + 0.5 * k_f) * mode_col
    z_local = lane // (2 * ROWS)
    px = (lane // ROWS) % 2
    r = lane % ROWS
    coarse_x = jnp.where(r < 8, r, r - ROWS)
    x = x_first + 2 * coarse_x + px
    x_angle = (x.astype(F32) + 0.5) * (math.pi / nx_total)
    z_angle = ((z_local + offset_ref[0]).astype(F32) + 0.5) * (math.pi / NZG)
    phase = z_angle * (k % 5).astype(F32) + x_angle * (1 + k % 4).astype(F32) + 0.7 * k_f
    x_ok = (r < 8) | (r >= 12)
    ones = jnp.where(x_ok & (x >= 0) & (x < nx_total), 1.0, 0.0)
    left = jnp.concatenate([amplitude * jnp.cos(phase), -amplitude * jnp.sin(phase)], 0)
    inside_x = lax.dot_general(ones, jnp.ones((modes, LANES), F32), (((0,), (0,)), ((), ())), preferred_element_type=F32)
    y_mode = (1 + (k // 4) % 4).astype(F32)
    for py in range(2):
        coarse_y = jnp.where(lane < half_y + 4, lane, lane - LANES)
        y = y_first + 2 * coarse_y + py
        y_angle = (y.astype(F32) + 0.5) * (math.pi / ny_total) * y_mode
        right = jnp.concatenate([jnp.cos(y_angle), jnp.sin(y_angle)], 0)
        log_kappa = lax.dot_general(
            left, right, (((0,), (0,)), ((), ())), precision=lax.Precision.HIGHEST, preferred_element_type=F32
        )
        y_full = y[0:1, :]
        lane_full = lane[0:1, :]
        y_ok = (lane_full < half_y + 4) | (lane_full >= LANES - 4)
        y_ok = y_ok & (y_full >= 0) & (y_full < ny_total)
        value = jnp.where((inside_x > 0.5) & y_ok, jnp.exp(0.5 * log_kappa), 0.0)
        for group in range(8):
            out_ref[group // 2, group % 2, py] = value[group * ROWS : (group + 1) * ROWS]


def select_columns(width):
    half = width // 2
    column = iota((width, 2 * LANES), 1)
    own = iota((width, 2 * LANES), 0)
    parity, k = column // LANES, column % LANES
    pick_own = jnp.where((k < half) & (own == 2 * k + parity), 1.0, 0.0).astype(BF16)
    strip = iota((2 * HALO, 2 * LANES), 0)
    column = iota((2 * HALO, 2 * LANES), 1)
    parity, k = column // LANES, column % LANES
    k = jnp.where(k >= LANES - 4, k - LANES, k)
    fine = jnp.where(strip < HALO, strip - HALO, strip - HALO + width)
    wanted = ((k < 0) | (k >= half)) & (k < half + 4)
    pick_strip = jnp.where(wanted & (fine == 2 * k + parity), 1.0, 0.0).astype(BF16)
    return pick_own, pick_strip


def exact_pick(values, pick, dims):
    total = None
    rest = values
    for _ in range(3):
        part = rest.astype(BF16)
        rest = rest - part.astype(F32)
        term = lax.dot_general(part, pick, (dims, ((), ())), preferred_element_type=F32)
        total = term if total is None else total + term
    return total


class Lazy:
    def __init__(self, rule):
        self.rule, self.known = rule, {}

    def __call__(self, *key):
        if key not in self.known:
            self.known[key] = self.rule(*key)
        return self.known[key]


def plus(*terms):
    total = None
    for term in terms:
        if term is not None:
            total = term if total is None else total + term
    return total


def times(left, right):
    return None if left is None or right is None else left * right


def minus(left, right):
    if right is None:
        return left
    return -right if left is None else left - right


def shift_x(value, steps):
    return None if value is None else pltpu.roll(value, (-steps) % ROWS, 0)


def shift_y(value, steps):
    return None if value is None else pltpu.roll(value, (-steps) % LANES, 1)


def main_body(field_ref, own_ref, near_ref, far_ref, stencil_ref, solution_ref, wide_ref):
    width_y = own_ref.shape[1]
    n_rows = own_ref.shape[0] - 4 * HALO
    groups = n_rows // HALO
    pick_own, pick_strip = select_columns(width_y)
    even_block = lax.axis_index("gx") % 2 == 0
    near, far = near_ref[...], far_ref[...]
    blocks = (own_ref[...], jnp.where(even_block, near, far), jnp.where(even_block, far, near))
    for g in range(groups):
        for py in range(2):
            wide_ref[g, py, 16:24, :] = jnp.zeros((8, LANES), F32)
    for block, place in zip(blocks, (0, 8, 24)):
        spread = exact_pick(block[:n_rows], pick_own, ((1,), (0,)))
        strips = jnp.concatenate([block[n_rows : n_rows + HALO], block[n_rows + 2 * HALO : n_rows + 3 * HALO]], 0)
        rest = jnp.concatenate([block[n_rows + HALO : n_rows + 2 * HALO], block[n_rows + 3 * HALO :]], 0)
        border = jnp.concatenate(
            [exact_pick(strips, pick_strip, ((0,), (0,))), exact_pick(rest, pick_strip, ((0,), (0,)))[: n_rows - LANES]], 0
        )
        spread = spread + border
        for g in range(groups):
            for py in range(2):
                wide_ref[g, py, place : place + 8, :] = spread[8 * g : 8 * g + 8, LANES * py : LANES * (py + 1)]

    planes = 2

    def base(kind, z, px, py):
        return wide_ref[4 * kind + z, py, pl.ds(px, ROWS, stride=2), :]

    s = Lazy(lambda z, px, py: field_ref[z, px, py])

    def face(axis, z, px, py):
        here = s(z, px, py)
        if axis == "x":
            there = s(z, 1, py) if px == 0 else shift_x(s(z, 0, py), 1)
            return base(0, z, px, py) * (here * there)
        if axis == "y":
            there = s(z, px, 1) if py == 0 else shift_y(s(z, px, 0), 1)
            return base(1, z, px, py) * (here * there)
        if z < 0 or z + 1 >= 2 * planes:
            return None
        return base(2, z, px, py) * (here * s(z + 1, px, py))

    face = Lazy(face)
    mass = Lazy(lambda z, px, py: base(3, z, px, py) * (s(z, px, py) * s(z, px, py)))

    def pair(axis, z, px, py):
        if axis == "x":
            lower = face("x", z, 0, py) if px else shift_x(face("x", z, 1, py), -1)
        elif axis == "y":
            lower = face("y", z, px, 0) if py else shift_y(face("y", z, px, 1), -1)
        else:
            lower = face("z", z - 1, px, py)
        return plus(face(axis, z, px, py), lower)

    pair = Lazy(pair)

    def inverse(z, px, py):
        total = mass(z, px, py)
        for axis, odd in (("x", px), ("y", py), ("z", z % 2)):
            if odd:
                total = total + pair(axis, z, px, py)
        return 1.0 / jnp.where(s(z, px, py) > 0.0, total, 1.0)

    inverse = Lazy(inverse)

    def w_x(i, a):
        return None if not 0 <= i < planes else inverse(2 * i, 1, 0) * face("x", 2 * i, a, 0)

    def w_y(i, b):
        return None if not 0 <= i < planes else inverse(2 * i, 0, 1) * face("y", 2 * i, 0, b)

    def w_z(i, c):
        return times(inverse(2 * i + 1, 0, 0), face("z", 2 * i + c, 0, 0))

    w_x, w_y, w_z = Lazy(w_x), Lazy(w_y), Lazy(w_z)
    w_x_up = Lazy(lambda i, a: shift_y(w_x(i, a), 1))
    w_y_up = Lazy(lambda i, b: shift_x(w_y(i, b), 1))
    w_z_upx = Lazy(lambda i, c: shift_x(w_z(i, c), 1))
    w_z_upy = Lazy(lambda i, c: shift_y(w_z(i, c), 1))

    def w_xy(i, a, b):
        if not 0 <= i < planes:
            return None
        z = 2 * i
        return inverse(z, 1, 1) * (
            face("x", z, a, 1) * (w_y_up(i, b) if a else w_y(i, b)) + face("y", z, 1, b) * (w_x_up(i, a) if b else w_x(i, a))
        )

    def w_xz(i, a, c):
        z = 2 * i + 1
        return times(
            inverse(z, 1, 0),
            plus(times(face("x", z, a, 0), w_z_upx(i, c) if a else w_z(i, c)), times(face("z", 2 * i + c, 1, 0), w_x(i + c, a))),
        )

    def w_yz(i, b, c):
        z = 2 * i + 1
        return times(
            inverse(z, 0, 1),
            plus(times(face("y", z, 0, b), w_z_upy(i, c) if b else w_z(i, c)), times(face("z", 2 * i + c, 0, 1), w_y(i + c, b))),
        )

    w_xy, w_xz, w_yz = Lazy(w_xy), Lazy(w_xz), Lazy(w_yz)
    w_yz_up = Lazy(lambda i, b, c: shift_x(w_yz(i, b, c), 1))
    w_xz_up = Lazy(lambda i, a, c: shift_y(w_xz(i, a, c), 1))

    def w_xyz(i, a, b, c):
        z = 2 * i + 1
        if not 0 <= i < planes or not 0 <= i + c < planes:
            return None
        return inverse(z, 1, 1) * (
            face("x", z, a, 1) * (w_yz_up(i, b, c) if a else w_yz(i, b, c))
            + face("y", z, 1, b) * (w_xz_up(i, a, c) if b else w_xz(i, a, c))
            + face("z", 2 * i + c, 1, 1) * w_xy(i + c, a, b)
        )

    w_xyz = Lazy(w_xyz)

    low_x = Lazy(lambda i, b, c, a: shift_x(times(face("x", 2 * i + 1, 1, 1), w_xyz(i, a, b, c)), -1))
    low_y = Lazy(lambda i, a, c, b: shift_y(times(face("y", 2 * i + 1, 1, 1), w_xyz(i, a, b, c)), -1))

    def t_xy(i, a, b, dz):
        z = 2 * i
        row = None
        if dz == 0:
            row = times(pair("z", z, 1, 1), w_xy(i, a, b))
        if dz >= 0:
            row = minus(row, times(face("z", z, 1, 1), w_xyz(i, a, b, dz)))
        if dz <= 0:
            row = minus(row, times(face("z", z - 1, 1, 1), w_xyz(i - 1, a, b, dz + 1)))
        return minus(w_xy(i, a, b) if dz == 0 else None, times(inverse(z, 1, 1), row))

    def t_xz(i, a, c, dy):
        z = 2 * i + 1
        if not 0 <= i < planes or not 0 <= i + c < planes:
            return None
        row = None
        if dy == 0:
            row = times(pair("y", z, 1, 0), w_xz(i, a, c))
        if dy >= 0:
            row = minus(row, times(face("y", z, 1, 0), w_xyz(i, a, dy, c)))
        if dy <= 0:
            row = minus(row, low_y(i, a, c, dy + 1))
        return minus(w_xz(i, a, c) if dy == 0 else None, times(inverse(z, 1, 0), row))

    def t_yz(i, b, c, dx):
        z = 2 * i + 1
        if not 0 <= i < planes or not 0 <= i + c < planes:
            return None
        row = None
        if dx == 0:
            row = times(pair("x", z, 0, 1), w_yz(i, b, c))
        if dx >= 0:
            row = minus(row, times(face("x", z, 0, 1), w_xyz(i, dx, b, c)))
        if dx <= 0:
            row = minus(row, low_x(i, b, c, dx + 1))
        return minus(w_yz(i, b, c) if dx == 0 else None, times(inverse(z, 0, 1), row))

    t_xy, t_xz, t_yz = Lazy(t_xy), Lazy(t_xz), Lazy(t_yz)

    def t_x(i, a, dy, dz):
        z = 2 * i
        row = None
        if dy == 0 and dz == 0:
            row = plus(pair("y", z, 1, 0), pair("z", z, 1, 0)) * w_x(i, a)
        if dy >= 0:
            row = minus(row, times(face("y", z, 1, 0), t_xy(i, a, dy, dz)))
        if dy <= 0:
            row = minus(row, shift_y(times(face("y", z, 1, 1), t_xy(i, a, dy + 1, dz)), -1))
        if dz >= 0:
            row = minus(row, times(face("z", z, 1, 0), t_xz(i, a, dz, dy)))
        if dz <= 0:
            row = minus(row, times(face("z", z - 1, 1, 0), t_xz(i - 1, a, dz + 1, dy)))
        return minus(w_x(i, a) if dy == 0 and dz == 0 else None, times(inverse(z, 1, 0), row))

    def t_y(i, b, dx, dz):
        z = 2 * i
        row = None
        if dx == 0 and dz == 0:
            row = plus(pair("x", z, 0, 1), pair("z", z, 0, 1)) * w_y(i, b)
        if dx >= 0:
            row = minus(row, times(face("x", z, 0, 1), t_xy(i, dx, b, dz)))
        if dx <= 0:
            row = minus(row, shift_x(times(face("x", z, 1, 1), t_xy(i, dx + 1, b, dz)), -1))
        if dz >= 0:
            row = minus(row, times(face("z", z, 0, 1), t_yz(i, b, dz, dx)))
        if dz <= 0:
            row = minus(row, times(face("z", z - 1, 0, 1), t_yz(i - 1, b, dz + 1, dx)))
        return minus(w_y(i, b) if dx == 0 and dz == 0 else None, times(inverse(z, 0, 1), row))

    def t_z(i, c, dx, dy):
        z = 2 * i + 1
        if not 0 <= i < planes or not 0 <= i + c < planes:
            return None
        row = None
        if dx == 0 and dy == 0:
            row = plus(pair("x", z, 0, 0), pair("y", z, 0, 0)) * w_z(i, c)
        if dx >= 0:
            row = minus(row, times(face("x", z, 0, 0), t_xz(i, dx, c, dy)))
        if dx <= 0:
            row = minus(row, shift_x(times(face("x", z, 1, 0), t_xz(i, dx + 1, c, dy)), -1))
        if dy >= 0:
            row = minus(row, times(face("y", z, 0, 0), t_yz(i, dy, c, dx)))
        if dy <= 0:
            row = minus(row, shift_y(times(face("y", z, 0, 1), t_yz(i, dy + 1, c, dx)), -1))
        return minus(w_z(i, c) if dx == 0 and dy == 0 else None, times(inverse(z, 0, 0), row))

    t_x, t_y, t_z = Lazy(t_x), Lazy(t_y), Lazy(t_z)

    def direct(i, dz, dx, dy):
        z = 2 * i
        row = None
        if dx == 0 and dy == 0 and dz == 0:
            row = plus(mass(z, 0, 0), pair("x", z, 0, 0), pair("y", z, 0, 0), pair("z", z, 0, 0))
        if dx >= 0:
            row = minus(row, times(face("x", z, 0, 0), t_x(i, dx, dy, dz)))
        if dx <= 0:
            row = minus(row, shift_x(times(face("x", z, 1, 0), t_x(i, dx + 1, dy, dz)), -1))
        if dy >= 0:
            row = minus(row, times(face("y", z, 0, 0), t_y(i, dy, dx, dz)))
        if dy <= 0:
            row = minus(row, shift_y(times(face("y", z, 0, 1), t_y(i, dy + 1, dx, dz)), -1))
        if dz >= 0:
            row = minus(row, times(face("z", z, 0, 0), t_z(i, dz, dx, dy)))
        if dz <= 0:
            row = minus(row, times(face("z", z - 1, 0, 0), t_z(i - 1, dz + 1, dx, dy)))
        return row

    def coarse(i, dz, dx, dy):
        if not 0 <= i + dz < planes:
            return None
        if (dz, dx, dy) >= (0, 0, 0):
            return direct(i, dz, dx, dy)
        return shift_y(shift_x(coarse(i + dz, -dz, -dx, -dy), dx), dy)

    coarse = Lazy(coarse)

    resid = Lazy(lambda z, px, py: base(4, z, px, py))
    odd_z = range(planes)
    q_xyz = [inverse(2 * i + 1, 1, 1) * resid(2 * i + 1, 1, 1) for i in odd_z] + [None]
    q_xy, q_xz, q_yz, q_x, q_y, q_z, rhs = [], [], [], [], [], [], []

    def side_x(z, py, value):
        return plus(times(face("x", z, 0, py), value), shift_x(times(face("x", z, 1, py), value), -1))

    def side_y(z, px, value):
        return plus(times(face("y", z, px, 0), value), shift_y(times(face("y", z, px, 1), value), -1))

    def side_z(z, px, py, values):
        i = z // 2
        return plus(times(face("z", z, px, py), values[i]), times(face("z", z - 1, px, py), values[i - 1] if i else None))

    for i in range(planes):
        z = 2 * i
        q_xy.append(inverse(z, 1, 1) * plus(resid(z, 1, 1), side_z(z, 1, 1, q_xyz)))
        q_xz.append(inverse(z + 1, 1, 0) * plus(resid(z + 1, 1, 0), side_y(z + 1, 1, q_xyz[i])))
        q_yz.append(inverse(z + 1, 0, 1) * plus(resid(z + 1, 0, 1), side_x(z + 1, 1, q_xyz[i])))
    for i in range(planes):
        z = 2 * i
        q_x.append(inverse(z, 1, 0) * plus(resid(z, 1, 0), side_y(z, 1, q_xy[i]), side_z(z, 1, 0, q_xz)))
        q_y.append(inverse(z, 0, 1) * plus(resid(z, 0, 1), side_x(z, 1, q_xy[i]), side_z(z, 0, 1, q_yz)))
        q_z.append(
            inverse(z + 1, 0, 0) * plus(resid(z + 1, 0, 0), side_x(z + 1, 0, q_xz[i]), side_y(z + 1, 0, q_yz[i]))
        )
    for i in range(planes):
        z = 2 * i
        rhs.append(plus(resid(z, 0, 0), side_x(z, 0, q_x[i]), side_y(z, 0, q_y[i]), side_z(z, 0, 0, q_z)))

    keep_x, keep_y = stencil_ref.shape[2:]
    for i in range(planes):
        for dz in (-1, 0, 1):
            for dx in (-1, 0, 1):
                for dy in (-1, 0, 1):
                    value = coarse(i, dz, dx, dy)
                    number = 9 * (dz + 1) + 3 * (dx + 1) + dy + 1
                    if value is None:
                        stencil_ref[number, i] = jnp.zeros((keep_x, keep_y), F32)
                    else:
                        stencil_ref[number, i] = value[:keep_x, :keep_y]

    scaled = []
    for i in range(planes):
        inside = s(2 * i, 0, 0) > 0.0
        scaled.append(jnp.where(inside, OMEGA / jnp.where(inside, coarse(i, 0, 0, 0), 1.0), 0.0))
    u = [scaled[i] * rhs[i] for i in range(planes)]
    for _ in range(SWEEPS - 1):
        moved = {}
        for i in range(planes):
            for dx in (-1, 0, 1):
                row = shift_x(u[i], dx) if dx else u[i]
                for dy in (-1, 0, 1):
                    moved[i, dx, dy] = shift_y(row, dy) if dy else row
        new = []
        for i in range(planes):
            total = None
            for dz in (-1, 0, 1):
                for dx in (-1, 0, 1):
                    for dy in (-1, 0, 1):
                        total = plus(total, times(coarse(i, dz, dx, dy), moved.get((i + dz, dx, dy))))
            new.append(u[i] + scaled[i] * (rhs[i] - total))
        u = new
    for i in range(planes):
        solution_ref[i] = u[i][:keep_x, :keep_y]


def ring(value, axis, steps):
    count = lax.axis_size(axis)
    return lax.ppermute(value, axis, [(i, (i + steps) % count) for i in range(count)])


def swap(value, axis, first):
    count = lax.axis_size(axis)
    partner = list(range(count))
    for i in range(first, count - 1, 2):
        partner[i], partner[i + 1] = i + 1, i
    return lax.ppermute(value, axis, list(enumerate(partner)))


def on_device(base_cond, base_mass, fine_residual, point_index, gen_vector, z_offset):
    plane_count, width_x, width_y = base_mass.shape
    nx_total = width_x * lax.axis_size("gx")
    ny_total = width_y * lax.axis_size("gy")
    strip = jax.ShapeDtypeStruct((2 * HALO, LANES), F32)
    low, high = pl.pallas_call(strips_body, out_shape=(strip, strip), name="strips")(base_cond, base_mass, fine_residual)
    from_below = ring(high, "gy", 1)
    from_above = ring(low, "gy", -1)
    smem = pl.BlockSpec(memory_space=pltpu.SMEM)
    vmem = pl.BlockSpec(memory_space=pltpu.VMEM)
    field = pl.pallas_call(
        lambda *refs: field_body(nx_total, ny_total, width_x, width_y, *refs),
        out_shape=jax.ShapeDtypeStruct((plane_count, 2, 2, ROWS, LANES), F32),
        in_specs=[smem, smem, vmem],
        out_specs=vmem,
        name="field",
    )(point_index, z_offset, gen_vector.reshape(1, -1))
    own = jnp.concatenate(
        [
            base_cond.reshape(-1, width_y),
            base_mass.reshape(-1, width_y),
            fine_residual.reshape(-1, width_y),
            from_below,
            from_above,
        ],
        0,
    )
    far = swap(own, "gx", 1)
    near = swap(own, "gx", 0)
    groups = 5 * plane_count
    return pl.pallas_call(
        main_body,
        out_shape=(
            jax.ShapeDtypeStruct((27, plane_count // 2, width_x // 2, width_y // 2), F32),
            jax.ShapeDtypeStruct((plane_count // 2, width_x // 2, width_y // 2), F32),
        ),
        scratch_shapes=[pltpu.VMEM((groups, 2, 2 * ROWS, LANES), F32)],
        name="galerkin",
    )(field, own, near, far)


def solution(mesh):
    return jax.shard_map(
        on_device,
        mesh=mesh,
        in_specs=(
            P(None, None, "gx", "gy"),
            P(None, "gx", "gy"),
            P("parts", "gx", "gy"),
            P("parts"),
            P(),
            P(),
        ),
        out_specs=(P(None, "parts", "gx", "gy"), P("parts", "gx", "gy")),
        check_vma=False,
    )
```

time: 197 us -> 20.6 us (0.10)
  starting transfers between devices: 78.7 us -> 7.16 us
  waiting for transfers between devices: 47.9 us -> 1.84 us
  other arithmetic: 29 us -> 0 us
  between operations: 23 us -> 1.97 us
  local copies, waits for them, and re-layouts: 17.3 us -> 2.71 us
  Pallas kernels: 0 us -> 6.49 us
    ppermute x32 -> x4, starting transfers between devices: 78.7 us -> 7.16 us  [the longest x2 4.55 us: swap(): return lax.ppermute(value, axis, list(enumerate(partner)))]
    ppermute x32 -> x4, waiting for transfers between devices: 47.9 us -> 1.84 us  [the longest x2 1.84 us: ring(): lax.ppermute(value, axis, [(i, (i + steps) % count) for i in range(count)])]
    slice x26 -> x0, local copies, waits for them, and re-layouts: 12.3 us -> none  [the longest x1 8.47 us: on_device(): restricted[:, ::2, margin:margin + width_x:2, margin:margin + width_y:2]]
    select_n x27 -> x0, other arithmetic: 12.1 us -> none  [the longest x1 4.44 us: effective(): jnp.where(open_x, base_cond[0] * jnp.exp(0.5 * (log_here + log_east)), 0.0)]
    add x12 -> x0, other arithmetic: 6.61 us -> none  [the longest x1 2.19 us: weights(): diagonal = mass_term + pair_x + pair_y + pair_z]
    pallas_call x0 -> x3, Pallas kernels: none -> 6.49 us  [the longest x1 2.9 us: on_device(): pl.pallas_call(main_body, out_shape=(jax.ShapeDtypeStruct((27, plane_coun...]
    concatenate x15 -> x0, other arithmetic: 3.24 us -> none  [the longest x3 2.36 us: assemble(): joined = jnp.concatenate([side, column], values.ndim - 1)]
    another operation x16 -> x0, other arithmetic: 2.98 us -> none  [the longest x1 2.64 us: effective(): return jnp.stack([cond_x, cond_y, cond_z, mass_term])]
  transfers between devices with their start and end apart: 32 -> 4, of which waited for: 15 -> 1; matrix products, arithmetic and copies ran while one was open for 5% -> 0% of each run, Pallas kernels for 0% -> 9%
where the time goes in v1:
time: 20.6 us; the launch traced here: 20.2 us
  starting transfers between devices  7.16 us (35%)
  Pallas kernels  6.49 us (32%)
  local copies, waits for them, and re-layouts  2.71 us (13%)
  between operations  1.97 us (10%)
  waiting for transfers between devices  1.84 us (9%)
    ppermute x2, starting transfers between devices, swap(): return lax.ppermute(value, axis, list(enumerate(partner)))  4.55 us
    pallas_call x1, Pallas kernels, on_device(): pl.pallas_call(main_body, out_shape=(jax.ShapeDtypeStruct((27, plane_coun...  2.9 us
    unnamed x16, local copies, waits for them, and re-layouts  2.71 us
    ppermute x2, starting transfers between devices, ring(): lax.ppermute(value, axis, [(i, (i + steps) % count) for i in range(count)])  2.6 us
    ppermute x2, waiting for transfers between devices, ring(): lax.ppermute(value, axis, [(i, (i + steps) % count) for i in range(count)])  1.84 us
    pallas_call x1, Pallas kernels, on_device(): pl.pallas_call(strips_body, out_shape=(strip, strip), name='strips')  1.83 us
    pallas_call x1, Pallas kernels, on_device(): pl.pallas_call(lambda *refs: field_body(nx_total, ny_total, width_x, widt...  1.76 us
  transfers between devices with their start and end apart: 4, of which 1 were waited for; matrix products, arithmetic and copies ran while one was open for 0% of the time, Pallas kernels for 9%

profile of v1, /device:TPU:1, one launch (start us, length us, event | category | flops | bytes accessed | tf_op | source)
XLA Modules:
  0.0 20.2 jit_solution(10872308157862576311)
XLA Ops:
  0.6 0.0 copy-start.1
  0.6 1.8 %strips.1 = (f32[16,128]{1,0:T(8,128)}, f32[16,128]{1,0:T(8,128)}) custom-call(f32[3,4,8,128]{3,2,1,0:T(8,128)} %cond_ref.1, f32[4,8,128]{2,1,0:T(8,128)} %mass_ref.1, f32[4,8,128]{2,1,0:T(8,128)} %resid_ref.1), custom_call_target="tpu_custom_call" | custom-call | tf_op jit(solution)/shard_map/strips/pallas_call | solution.py:470
  2.5 2.6 %collective-permute-start = (f32[16,128]{1,0:T(8,128)}, f32[16,128]{1,0:T(8,128)S(1)}, u32[]{:S(2)}, u32[]{:S(2)}) collective-permute-start(f32[16,128]{1,0:T(8,128)} %get-tuple-element.4), channel_id=1, source_target_pairs={{0,1},{1,2},{2,3},{3,0},{4,5},{5,6},{6,7},{7,4},{8,9},{9,10},{10,1... | collective-permute-start | bytes 24584 | tf_op jit(solution)/shard_map/ppermute | solution.py:454
  5.1 0.0 collective-permute-start.1
  5.1 0.0 copy-done.1
  5.1 0.0 copy-start.4
  5.1 0.7 %copy-done.4 = f32[4,8,128]{2,1,0:T(8,128)S(1)} copy-done((f32[4,8,128]{2,1,0:T(8,128)S(1)}, f32[4,8,128]{2,1,0:T(8,128)}, u32[]{:S(2)}) %copy-start.4) | copy-done | bytes 16408
  5.8 0.0 copy-start.5
  5.8 0.7 %copy-done.5 = f32[4,8,128]{2,1,0:T(8,128)S(1)} copy-done((f32[4,8,128]{2,1,0:T(8,128)S(1)}, f32[4,8,128]{2,1,0:T(8,128)}, u32[]{:S(2)}) %copy-start.5) | copy-done | bytes 16408
  6.5 0.0 collective-permute-done
  6.5 1.8 %collective-permute-done.1 = f32[16,128]{1,0:T(8,128)S(1)} collective-permute-done((f32[16,128]{1,0:T(8,128)}, f32[16,128]{1,0:T(8,128)S(1)}, u32[]{:S(2)}, u32[]{:S(2)}) %collective-permute-start.1) | collective-permute-done | bytes 8224 | tf_op jit(solution)/shard_map/ppermute | solution.py:454
  8.4 0.0 copy-start
  8.4 0.7 %collective-permute-start.3 = (f32[192,128]{1,0:T(8,128)S(1)}, f32[192,128]{1,0:T(8,128)S(1)}, u32[]{:S(2)}, u32[]{:S(2)}) collective-permute-start(f32[192,128]{1,0:T(8,128)S(1)} %constant_dynamic-update-slice_fusion.own_ref), channel_id=1, source_target_pairs={{0,0},{4,8},{8,4},{12,12},{1,1},{5,9},{9,5},{13,13},{2,2},{6,10},{... | collective-permute-start | bytes 294920 | tf_op jit(solution)/shard_map/ppermute | solution.py:462
  9.0 3.9 %collective-permute-start.2 = (f32[192,128]{1,0:T(8,128)S(1)}, f32[192,128]{1,0:T(8,128)S(1)}, u32[]{:S(2)}, u32[]{:S(2)}) collective-permute-start(f32[192,128]{1,0:T(8,128)S(1)} %constant_dynamic-update-slice_fusion.own_ref), channel_id=1, source_target_pairs={{0,4},{4,0},{8,12},{12,8},{1,5},{5,1},{9,13},{13,9},{2,6},{6,2},{1... | collective-permute-start | bytes 294920 | tf_op jit(solution)/shard_map/ppermute | solution.py:462
  14.2 1.8 %field.1.field_ref = f32[4,2,2,16,128]{4,3,2,1,0:T(8,128)} custom-call(s32[1]{0:T(128)S(6)} %copy.12.refs_0_, s32[1]{0:T(128)S(6)} %copy.13.refs_1_, s32[1,32]{1,0:T(1,128)} %bitcast.7), custom_call_target="tpu_custom_call" | custom-call | tf_op jit(solution)/shard_map/field/pallas_call | solution.py:475
  16.0 0.0 collective-permute-done.3.far_ref
  16.0 0.0 copy-start.2
  16.0 0.0 collective-permute-done.2.near_ref
  16.0 0.0 copy-done
  16.0 0.6 %copy-done.2 = f32[192,128]{1,0:T(8,128)} copy-done((f32[192,128]{1,0:T(8,128)}, f32[192,128]{1,0:T(8,128)S(1)}, u32[]{:S(2)}) %copy-start.2) | copy-done | bytes 98328
  16.6 0.0 copy-start.3
  16.6 0.6 %copy-done.3 = f32[192,128]{1,0:T(8,128)} copy-done((f32[192,128]{1,0:T(8,128)}, f32[192,128]{1,0:T(8,128)S(1)}, u32[]{:S(2)}) %copy-start.3) | copy-done | bytes 98328
  17.3 2.9 %galerkin.1 = (f32[27,2,4,64]{3,2,1,0:T(4,128)}, f32[2,4,64]{2,1,0:T(4,128)}) custom-call(f32[4,2,2,16,128]{4,3,2,1,0:T(8,128)} %field.1.field_ref, f32[192,128]{1,0:T(8,128)} %copy-done, f32[192,128]{1,0:T(8,128)} %copy-done.3, f32[192,128]{1,0:T(8,128)} %copy-done.2), custom_call_target="tpu_custom_call" | custom-call | tf_op jit(solution)/shard_map/galerkin/pallas_call | solution.py:495
  (5 shorter events, 0.0 us)
Async XLA Ops:
  0.6 4.4 %copy-start.1 = (f32[3,4,8,128]{3,2,1,0:T(8,128)S(1)}, f32[3,4,8,128]{3,2,1,0:T(8,128)}, u32[]{:S(2)}) copy-start(f32[3,4,8,128]{3,2,1,0:T(8,128)} %cond_ref.1) | copy-start | bytes 147460
  2.5 4.0 %collective-permute-start = (f32[16,128]{1,0:T(8,128)}, f32[16,128]{1,0:T(8,128)S(1)}, u32[]{:S(2)}, u32[]{:S(2)}) collective-permute-start(f32[16,128]{1,0:T(8,128)} %get-tuple-element.4), channel_id=1, source_target_pairs={{0,1},{1,2},{2,3},{3,0},{4,5},{5,6},{6,7},{7,4},{8,9},{9,10},{10,1... | collective-permute-start | bytes 24584 | tf_op jit(solution)/shard_map/ppermute | solution.py:454
  5.1 3.3 %collective-permute-start.1 = (f32[16,128]{1,0:T(8,128)}, f32[16,128]{1,0:T(8,128)S(1)}, u32[]{:S(2)}, u32[]{:S(2)}) collective-permute-start(f32[16,128]{1,0:T(8,128)} %get-tuple-element.5), channel_id=1, source_target_pairs={{0,3},{1,0},{2,1},{3,2},{4,7},{5,4},{6,5},{7,6},{8,11},{9,8},{10,9... | collective-permute-start | bytes 24584 | tf_op jit(solution)/shard_map/ppermute | solution.py:454
  5.1 0.7 %copy-start.4 = (f32[4,8,128]{2,1,0:T(8,128)S(1)}, f32[4,8,128]{2,1,0:T(8,128)}, u32[]{:S(2)}) copy-start(f32[4,8,128]{2,1,0:T(8,128)} %mass_ref.1) | copy-start | bytes 49156
  5.8 0.7 %copy-start.5 = (f32[4,8,128]{2,1,0:T(8,128)S(1)}, f32[4,8,128]{2,1,0:T(8,128)}, u32[]{:S(2)}) copy-start(f32[4,8,128]{2,1,0:T(8,128)} %resid_ref.1) | copy-start | bytes 49156
  8.4 7.6 %copy-start = (f32[192,128]{1,0:T(8,128)}, f32[192,128]{1,0:T(8,128)S(1)}, u32[]{:S(2)}) copy-start(f32[192,128]{1,0:T(8,128)S(1)} %constant_dynamic-update-slice_fusion.own_ref) | copy-start | bytes 294916
  8.4 7.6 %collective-permute-start.3 = (f32[192,128]{1,0:T(8,128)S(1)}, f32[192,128]{1,0:T(8,128)S(1)}, u32[]{:S(2)}, u32[]{:S(2)}) collective-permute-start(f32[192,128]{1,0:T(8,128)S(1)} %constant_dynamic-update-slice_fusion.own_ref), channel_id=1, source_target_pairs={{0,0},{4,8},{8,4},{12,12},{1,1},{5,9},{9,5},{13,13},{2,2},{6,10},{... | collective-permute-start | bytes 294920 | tf_op jit(solution)/shard_map/ppermute | solution.py:462
  9.0 7.0 %collective-permute-start.2 = (f32[192,128]{1,0:T(8,128)S(1)}, f32[192,128]{1,0:T(8,128)S(1)}, u32[]{:S(2)}, u32[]{:S(2)}) collective-permute-start(f32[192,128]{1,0:T(8,128)S(1)} %constant_dynamic-update-slice_fusion.own_ref), channel_id=1, source_target_pairs={{0,4},{4,0},{8,12},{12,8},{1,5},{5,1},{9,13},{13,9},{2,6},{6,2},{1... | collective-permute-start | bytes 294920 | tf_op jit(solution)/shard_map/ppermute | solution.py:462
  16.0 0.6 %copy-start.2 = (f32[192,128]{1,0:T(8,128)}, f32[192,128]{1,0:T(8,128)S(1)}, u32[]{:S(2)}) copy-start(f32[192,128]{1,0:T(8,128)S(1)} %collective-permute-done.3.far_ref) | copy-start | bytes 294916
  16.6 0.6 %copy-start.3 = (f32[192,128]{1,0:T(8,128)}, f32[192,128]{1,0:T(8,128)S(1)}, u32[]{:S(2)}) copy-start(f32[192,128]{1,0:T(8,128)S(1)} %collective-permute-done.2.near_ref) | copy-start | bytes 294916
